TPU v7x, 128 devices: a whole 4x4x4 slice. The times are simulated.
128 devices in a mesh: row: 8 (over y_lo, z), col: 16 (over x, y_hi, core).
Axes of the slice: x: 4, y: 4 (y_hi: 2, y_lo: 2; y = y_hi * 2 + y_lo), z: 4, core: 2. Of those that a mesh axis runs over, the one named last changes fastest.
Arguments:
- feats_one: bfloat16 [65536, 256], P(('row', 'col')), may hold values from -6 to 6
- feats_two: bfloat16 [65536, 256], P(('row', 'col')), may hold values from -6 to 6
- target_view: bfloat16 [65536, 256], P(('row', 'col')), may hold values from -6 to 6
- negatives: int32 [65536], P(('row', 'col')), may hold values from 0 to 511
- weight_one: bfloat16 [256, 256], replicated, may hold values from -0.375 to 0.375
- weight_two: bfloat16 [256, 256], replicated, may hold values from -0.375 to 0.375
- block_tiles: bfloat16 [81920, 128, 128], P(('row', 'col')), may hold values from -0.15625 to 0.15625
- tile_rows: int32 [81920], P(('row', 'col')), may hold values from 0 to 31
- tile_cols: int32 [81920], P(('row', 'col')), may hold values from 0 to 31
- block_counts: int32 [128], P(('row', 'col')), may hold values from 80 to 640, as said below
- need_rows: int32 [128, 16, 2], P(('row', 'col')), may hold values from 0 to 3, as said below
Outputs:
- grad_hidden: bfloat16 [65536, 256], P(('row', 'col'))
- grad_first: float32 [256, 256], replicated
- grad_second: float32 [256, 256], replicated
Inputs may be any that keep to these rules, and one draw needn't show every extreme that they name: `need_rows`: for each owner and source, the 2 entries are distinct. `block_counts`: live tiles of one block list.
All inputs are finite; a program needn't handle non-finite values.
Results may differ from a plain program's by a relative error of at most 0.0063.
Values may be sent and summed in bfloat16 or wider, within the bound.
No kernel may reach another device: no remote copies, remote signals or barrier semaphores. Data moves between devices by JAX's collectives and lax.ppermute only.
A program may use at most 192 MiB of HBM per device.

v0:
```python
import math
import jax
import jax.numpy as jnp
from jax import lax
from jax.sharding import PartitionSpec as P


def silu_slope(values):
    sig = jax.nn.sigmoid(values)
    return sig * (1.0 + values * (1.0 - sig))


def column_product(left, right):
    return lax.dot_general(
        left, right, (((0,), (0,)), ((), ())), preferred_element_type=jnp.float32
    )


def on_device(
    feats_one,
    feats_two,
    target_view,
    negatives,
    weight_one,
    weight_two,
    block_tiles,
    tile_rows,
    tile_cols,
    block_counts,
    need_rows,
):
    node_dev, features = feats_two.shape
    capacity, tile_size = (block_tiles.shape[0], block_tiles.shape[1])
    sources = lax.axis_size("col")
    row_group = lax.axis_size("row")
    tiles_dev = node_dev // tile_size
    slot_count = need_rows.shape[2]
    col_count = row_group * tiles_dev
    inverse_root = 1.0 / math.sqrt(features)
    weight_norm = 1.0 / math.sqrt(node_dev * row_group * sources)
    pre_two = jnp.dot(feats_two, weight_two, preferred_element_type=jnp.float32)
    hidden = jax.nn.silu(pre_two)
    partner_rows = hidden[negatives]
    target_full = target_view.astype(jnp.float32)
    s_pos = jnp.sum(hidden * target_full, axis=-1) * inverse_root
    s_neg = jnp.sum(hidden * partner_rows, axis=-1) * inverse_root
    prob_pos = jax.nn.sigmoid(-s_pos)
    prob_neg = jax.nn.sigmoid(s_neg)
    grad_out = -prob_pos[:, None] * target_full + prob_neg[:, None] * partner_rows
    grad_out = grad_out + jax.ops.segment_sum(
        prob_neg[:, None] * hidden, negatives, num_segments=node_dev
    )
    dpre_two = (grad_out * silu_slope(pre_two)).astype(jnp.bfloat16)
    grad_second = column_product(feats_two, dpre_two)
    grad_second = lax.psum(grad_second, ("row", "col"))
    message = lax.dot_general(
        dpre_two, weight_two, (((1,), (1,)), ((), ())), preferred_element_type=jnp.float32
    ).astype(jnp.bfloat16)
    gathered = lax.all_gather(message, "col", axis=0, tiled=True)
    buffer_tiles = gathered.reshape(sources * tiles_dev, tile_size, features)
    need_flat = need_rows[0].reshape(-1)
    slot_ids = jnp.arange(sources * slot_count, dtype=jnp.int32)
    local_tile = jnp.sum(
        jnp.where(tile_rows[:, None] == slot_ids[None, :], need_flat[None, :], 0), axis=1
    )
    row_tile = tile_rows // slot_count * tiles_dev + local_tile
    block_len = 128
    rounds = capacity // block_len
    live = (jnp.arange(capacity, dtype=jnp.int32) < block_counts[0]).astype(jnp.float32)
    column_ids = jnp.arange(col_count, dtype=jnp.int32)

    def add_block(summed_tiles, pieces):
        tile_part, row_part, col_part, live_part = pieces
        gathered_rows = buffer_tiles[row_part]
        contrib = jnp.einsum(
            "ktu,ktf->kuf", tile_part, gathered_rows, preferred_element_type=jnp.float32
        )
        selector = jnp.where(col_part[:, None] == column_ids[None, :], live_part[:, None], 0.0)
        placed = jnp.einsum(
            "kc,kuf->cuf",
            selector,
            contrib,
            precision=lax.Precision.HIGHEST,
            preferred_element_type=jnp.float32,
        )
        return (summed_tiles + placed, None)

    start_tiles = jnp.zeros((col_count, tile_size, features), jnp.float32)
    summed_tiles, _ = lax.scan(
        add_block,
        start_tiles,
        (
            block_tiles.reshape(rounds, block_len, tile_size, tile_size),
            row_tile.reshape(rounds, block_len),
            tile_cols.reshape(rounds, block_len),
            live.reshape(rounds, block_len),
        ),
    )
    column_total = lax.psum_scatter(
        summed_tiles.reshape(col_count * tile_size, features),
        "row",
        scatter_dimension=0,
        tiled=True,
    )
    grad_hidden = column_total.astype(jnp.bfloat16)
    pre_one = jnp.dot(feats_one, weight_one, preferred_element_type=jnp.float32)
    dpre_one = (grad_hidden.astype(jnp.float32) * silu_slope(pre_one)).astype(jnp.bfloat16)
    grad_first = column_product(feats_one, dpre_one)
    grad_first = lax.psum(grad_first, ("row", "col"))
    return (grad_hidden, grad_first * weight_norm, grad_second * weight_norm)


def solution(mesh):
    return jax.shard_map(
        on_device,
        mesh=mesh,
        in_specs=(
            P(("row", "col"), None),
            P(("row", "col"), None),
            P(("row", "col"), None),
            P(("row", "col")),
            P(),
            P(),
            P(("row", "col"), None, None),
            P(("row", "col")),
            P(("row", "col")),
            P(("row", "col")),
            P(("row", "col"), None, None),
        ),
        out_specs=(P(("row", "col"), None), P(), P()),
        check_vma=False,
    )
```

profile of v0, /device:TPU:1, one launch (start us, length us, event | category | flops | bytes accessed | tf_op | source)
XLA Modules:
  0.0 544.5 jit_solution(12721467284938459450)
XLA Ops:
  7.2 0.0 copy-start
  7.2 0.0 copy-start.4
  7.2 0.0 all-gather.2.cloned.1.call-start
  7.2 1.0 copy-done
  8.2 1.2 fusion.22
  9.5 0.2 copy.43
  9.7 0.7 compare_select_fusion.1
  10.4 1.6 gather_fusion.1
  11.9 0.2 copy.44
  12.1 0.1 copy.42
  12.3 0.0 copy-start.2
  12.3 0.1 fusion.20
  12.5 0.2 broadcast_multiply_fusion
  12.6 0.2 copy.46
  12.8 0.2 copy.47
  13.1 3.5 scatter_fusion
  16.6 0.2 copy.48
  16.8 0.2 multiply_convert_fusion.1
  17.0 1.0 convolution_convert_fusion
  18.0 0.0 all-gather.2.cloned.1.call-update
  18.0 0.0 reduce-scatter.2.cloned.1.call-start
  18.1 0.0 copy-start.5
  18.1 0.0 copy-start.3
  18.1 27.9 %copy.40 = bf16[640,128,128]{1,2,0:T(8,128)(2,1)} copy(bf16[640,128,128]{2,1,0:T(8,128)(2,1)} %param.19) | data formatting | bytes 41943040 | tf_op args[6]
  46.0 0.1 copy.41
  46.1 0.1 broadcast_in_dim.48
  46.9 0.1 select_reduce_fusion
  47.0 30.8 %all-gather.2.cloned.1.call-done = bf16[8192,256]{1,0:T(8,128)(2,1)} async-done(((bf16[512,256]{1,0:T(8,128)(2,1)}), bf16[8192,256]{1,0:T(8,128)(2,1)}) %all-gather.2.cloned.1.call-update) | async-done | bytes 4194320 | tf_op jit(solution)/shard_map/all_gather | solution.py:59
  77.8 241.0 %while.11 = (s32[]{:T(128)}, f32[32,128,256]{2,0,1:T(8,128)}, s32[5,128]{1,0:T(8,128)}, f32[5,128]{1,0:T(8,128)S(1)}, bf16[5,128,128,128]{2,3,1,0:T(8,128)(2,1)}...) while((s32[]{:T(128)}, f32[32,128,256]{2,0,1:T(8,128)}, ...), condition=%wide.region_5.6_spmd.clone, body=%wide.region_4.5_spmd.clone.sunk | while | flops 2686461440 | bytes 71313008 | solution.py:89
  77.8 8.7 %gather_fusion = bf16[128,128,256]{2,1,0:T(8,128)(2,1)} fusion(bf16[64,128,256]{2,1,0:T(8,128)(2,1)} %get-tuple-element.172, s32[1024]{0:T(1024)S(1)} %pad_clamp_fusion.3), kind=kCustom, calls=%fused_computation.clone.clone.1 | custom fusion | bytes 16777728 | tf_op jit(solution)/shard_map/while/body/eval_jaxpr/gather | solution.py:74
  86.5 12.8 %fusion.55 = f32[128,128,256]{2,1,0:T(8,128)} fusion(bf16[128,128,256]{2,1,0:T(8,128)(2,1)} %gather_fusion, bf16[5,128,128,128]{2,3,1,0:T(8,128)(2,1)} %get-tuple-element.170, s32[]{:T(128)} %get-tuple-element.157), kind=kOutput, calls=%fused_computation.6.clone.1 | convolution fusion | flops 1073741824 | bytes 29360640 | tf_op jit(solution)/shard_map/while/body/eval_jaxpr/ktu,ktf->kuf/dot_general | solution.py:75
  99.4 0.7 fusion.57
  100.0 25.4 %select_add_fusion.2 = f32[32,128,256]{2,0,1:T(8,128)} fusion(f32[32,128,256]{2,0,1:T(8,128)} %get-tuple-element.158, pred[]{:T(512)S(6)} %compare.5, f32[128,128,256]{2,1,0:T(8,128)} %fusion.55, f32[128]{0:T(128)S(1)} %fusion.56, s32[128]{0:T(128)S(1)} %fusion.57), kind=kOutput, calls=%fused_computation.8.clone.1 | convolution fusion | flops 1612718080 | bytes 25166848 | tf_op jit(solution)/shard_map/while/body/eval_jaxpr/kc,kuf->cuf/dot_general | solution.py:79
  125.5 8.7 %gather_fusion = bf16[128,128,256]{2,1,0:T(8,128)(2,1)} fusion(bf16[64,128,256]{2,1,0:T(8,128)(2,1)} %get-tuple-element.172, s32[1024]{0:T(1024)S(1)} %pad_clamp_fusion.3), kind=kCustom, calls=%fused_computation.clone.clone.1 | custom fusion | bytes 16777728 | tf_op jit(solution)/shard_map/while/body/eval_jaxpr/gather | solution.py:74
  134.2 12.8 %fusion.55 = f32[128,128,256]{2,1,0:T(8,128)} fusion(bf16[128,128,256]{2,1,0:T(8,128)(2,1)} %gather_fusion, bf16[5,128,128,128]{2,3,1,0:T(8,128)(2,1)} %get-tuple-element.170, s32[]{:T(128)} %get-tuple-element.157), kind=kOutput, calls=%fused_computation.6.clone.1 | convolution fusion | flops 1073741824 | bytes 29360640 | tf_op jit(solution)/shard_map/while/body/eval_jaxpr/ktu,ktf->kuf/dot_general | solution.py:75
  147.1 0.7 fusion.57
  147.8 26.0 %select_add_fusion.2 = f32[32,128,256]{2,0,1:T(8,128)} fusion(f32[32,128,256]{2,0,1:T(8,128)} %get-tuple-element.158, pred[]{:T(512)S(6)} %compare.5, f32[128,128,256]{2,1,0:T(8,128)} %fusion.55, f32[128]{0:T(128)S(1)} %fusion.56, s32[128]{0:T(128)S(1)} %fusion.57), kind=kOutput, calls=%fused_computation.8.clone.1 | convolution fusion | flops 1612718080 | bytes 25166848 | tf_op jit(solution)/shard_map/while/body/eval_jaxpr/kc,kuf->cuf/dot_general | solution.py:79
  173.8 8.7 %gather_fusion = bf16[128,128,256]{2,1,0:T(8,128)(2,1)} fusion(bf16[64,128,256]{2,1,0:T(8,128)(2,1)} %get-tuple-element.172, s32[1024]{0:T(1024)S(1)} %pad_clamp_fusion.3), kind=kCustom, calls=%fused_computation.clone.clone.1 | custom fusion | bytes 16777728 | tf_op jit(solution)/shard_map/while/body/eval_jaxpr/gather | solution.py:74
  182.6 12.8 %fusion.55 = f32[128,128,256]{2,1,0:T(8,128)} fusion(bf16[128,128,256]{2,1,0:T(8,128)(2,1)} %gather_fusion, bf16[5,128,128,128]{2,3,1,0:T(8,128)(2,1)} %get-tuple-element.170, s32[]{:T(128)} %get-tuple-element.157), kind=kOutput, calls=%fused_computation.6.clone.1 | convolution fusion | flops 1073741824 | bytes 29360640 | tf_op jit(solution)/shard_map/while/body/eval_jaxpr/ktu,ktf->kuf/dot_general | solution.py:75
  195.4 0.7 fusion.57
  196.1 26.0 %select_add_fusion.2 = f32[32,128,256]{2,0,1:T(8,128)} fusion(f32[32,128,256]{2,0,1:T(8,128)} %get-tuple-element.158, pred[]{:T(512)S(6)} %compare.5, f32[128,128,256]{2,1,0:T(8,128)} %fusion.55, f32[128]{0:T(128)S(1)} %fusion.56, s32[128]{0:T(128)S(1)} %fusion.57), kind=kOutput, calls=%fused_computation.8.clone.1 | convolution fusion | flops 1612718080 | bytes 25166848 | tf_op jit(solution)/shard_map/while/body/eval_jaxpr/kc,kuf->cuf/dot_general | solution.py:79
  222.2 8.8 %gather_fusion = bf16[128,128,256]{2,1,0:T(8,128)(2,1)} fusion(bf16[64,128,256]{2,1,0:T(8,128)(2,1)} %get-tuple-element.172, s32[1024]{0:T(1024)S(1)} %pad_clamp_fusion.3), kind=kCustom, calls=%fused_computation.clone.clone.1 | custom fusion | bytes 16777728 | tf_op jit(solution)/shard_map/while/body/eval_jaxpr/gather | solution.py:74
  230.9 12.8 %fusion.55 = f32[128,128,256]{2,1,0:T(8,128)} fusion(bf16[128,128,256]{2,1,0:T(8,128)(2,1)} %gather_fusion, bf16[5,128,128,128]{2,3,1,0:T(8,128)(2,1)} %get-tuple-element.170, s32[]{:T(128)} %get-tuple-element.157), kind=kOutput, calls=%fused_computation.6.clone.1 | convolution fusion | flops 1073741824 | bytes 29360640 | tf_op jit(solution)/shard_map/while/body/eval_jaxpr/ktu,ktf->kuf/dot_general | solution.py:75
  243.7 0.7 fusion.57
  244.4 26.0 %select_add_fusion.2 = f32[32,128,256]{2,0,1:T(8,128)} fusion(f32[32,128,256]{2,0,1:T(8,128)} %get-tuple-element.158, pred[]{:T(512)S(6)} %compare.5, f32[128,128,256]{2,1,0:T(8,128)} %fusion.55, f32[128]{0:T(128)S(1)} %fusion.56, s32[128]{0:T(128)S(1)} %fusion.57), kind=kOutput, calls=%fused_computation.8.clone.1 | convolution fusion | flops 1612718080 | bytes 25166848 | tf_op jit(solution)/shard_map/while/body/eval_jaxpr/kc,kuf->cuf/dot_general | solution.py:79
  270.5 8.7 %gather_fusion = bf16[128,128,256]{2,1,0:T(8,128)(2,1)} fusion(bf16[64,128,256]{2,1,0:T(8,128)(2,1)} %get-tuple-element.172, s32[1024]{0:T(1024)S(1)} %pad_clamp_fusion.3), kind=kCustom, calls=%fused_computation.clone.clone.1 | custom fusion | bytes 16777728 | tf_op jit(solution)/shard_map/while/body/eval_jaxpr/gather | solution.py:74
  279.2 12.8 %fusion.55 = f32[128,128,256]{2,1,0:T(8,128)} fusion(bf16[128,128,256]{2,1,0:T(8,128)(2,1)} %gather_fusion, bf16[5,128,128,128]{2,3,1,0:T(8,128)(2,1)} %get-tuple-element.170, s32[]{:T(128)} %get-tuple-element.157), kind=kOutput, calls=%fused_computation.6.clone.1 | convolution fusion | flops 1073741824 | bytes 29360640 | tf_op jit(solution)/shard_map/while/body/eval_jaxpr/ktu,ktf->kuf/dot_general | solution.py:75
  292.1 0.7 fusion.57
  292.8 26.0 %select_add_fusion.2 = f32[32,128,256]{2,0,1:T(8,128)} fusion(f32[32,128,256]{2,0,1:T(8,128)} %get-tuple-element.158, pred[]{:T(512)S(6)} %compare.5, f32[128,128,256]{2,1,0:T(8,128)} %fusion.55, f32[128]{0:T(128)S(1)} %fusion.56, s32[128]{0:T(128)S(1)} %fusion.57), kind=kOutput, calls=%fused_computation.8.clone.1 | convolution fusion | flops 1612718080 | bytes 25166848 | tf_op jit(solution)/shard_map/while/body/eval_jaxpr/kc,kuf->cuf/dot_general | solution.py:79
  318.8 5.9 %copy.49 = f32[32,128,256]{1,0,2:T(8,128)} copy(f32[32,128,256]{2,0,1:T(8,128)} %get-tuple-element.45) | data formatting | bytes 8388608 | tf_op jit(solution)/shard_map/while | solution.py:89
  324.8 8.0 %copy.62 = f32[32,8,32,128]{3,1,2,0:T(8,128)} copy(f32[32,8,32,128]{3,2,1,0:T(8,128)} %bitcast.62) | data formatting | bytes 8388608
  332.8 0.0 reduce-scatter.2.cloned.1.call-update
  332.8 0.0 all-reduce.3.cloned.1.call-start
  332.8 0.9 convolution_bitcast_fusion
  333.8 50.9 %reduce-scatter.2.cloned.1.call-done = f32[512,256]{0,1:T(8,128)} async-done(((f32[4096,256]{0,1:T(8,128)}), f32[512,256]{0,1:T(8,128)}) %reduce-scatter.2.cloned.1.call-update) | async-done | bytes 524304 | tf_op jit(solution)/shard_map/reduce_scatter | solution.py:99
  384.7 1.1 convert_element_type.26
  385.8 1.2 convolution_bitcast_fusion.1
  387.0 0.0 all-reduce.3.cloned.1.call-update
  387.0 0.8 copy.52
  387.9 146.5 %all-reduce.3.cloned.1.call-done = (f32[256,256]{0,1:T(8,128)}, f32[256,256]{0,1:T(8,128)}) async-done(((f32[256,256]{0,1:T(8,128)}, f32[256,256]{0,1:T(8,128)}), (f32[256,256]{0,1:T(8,128)}, f32[256,256]{0,1:T(8,128)})) %all-reduce.3.cloned.1.call-update) | async-done | bytes 524304 | tf_op jit(solution)/shard_map/psum | solution.py:109
  534.4 1.0 broadcast_multiply_fusion.2
  535.3 0.8 copy.53
  536.2 1.0 broadcast_multiply_fusion.1
  537.1 0.8 copy.54
  (30 shorter events, 0.2 us)
Async XLA Ops:
  7.2 1.0 copy-start
  7.2 5.9 %copy-start.4 = (s32[512]{0:T(512)S(1)}, s32[512]{0:T(512)}, u32[]{:S(2)}) copy-start(s32[512]{0:T(512)} %param.16) | copy-start | bytes 6148
  7.2 4.9 copy-start.1
  7.2 70.6 %all-gather.2.cloned.1.call-start = ((), (), s32[]{:S(2)}) async-start(), calls=%async_computation.1 | async-start | bytes 4456448 | tf_op jit(solution)/shard_map/all_gather | solution.py:59
  12.3 4.7 copy-start.2
  18.0 366.7 %reduce-scatter.2.cloned.1.call-start = ((), (), s32[]{:S(2)}) async-start(), calls=%async_computation.2 | async-start | bytes 4718592 | tf_op jit(solution)/shard_map/reduce_scatter | solution.py:99
  18.1 27.9 %copy-start.5 = (s32[1,16,2]{1,2,0:T(2,128)S(1)}, s32[1,16,2]{1,2,0:T(2,128)}, u32[]{:S(2)}) copy-start(s32[1,16,2]{1,2,0:T(2,128)} %param.23) | copy-start | bytes 388
  18.1 28.8 %copy-start.3 = (s32[640]{0:T(1024)S(1)}, s32[640]{0:T(1024)}, u32[]{:S(2)}) copy-start(s32[640]{0:T(1024)} %param.20) | copy-start | bytes 7684
  324.8 61.0 %copy-start.6 = (bf16[512,256]{1,0:T(8,128)(2,1)S(1)}, bf16[512,256]{1,0:T(8,128)(2,1)}, u32[]{:S(2)}) copy-start(bf16[512,256]{1,0:T(8,128)(2,1)} %param.13) | copy-start | bytes 786436
  324.8 61.0 %copy-start.7 = (bf16[256,256]{1,0:T(8,128)(2,1)S(1)}, bf16[256,256]{1,0:T(8,128)(2,1)}, u32[]{:S(2)}) copy-start(bf16[256,256]{1,0:T(8,128)(2,1)} %param.17) | copy-start | bytes 393220
  332.8 201.6 %all-reduce.3.cloned.1.call-start = ((), (), s32[]{:S(2)}) async-start(), calls=%async_computation.3 | async-start | bytes 1048576 | tf_op jit(solution)/shard_map/psum | solution.py:109
Sparse Core Ops, SparseCore 0:
  18.2 59.5 all-gather.1
  332.9 51.7 reduce-scatter.1
  390.2 144.0 all-reduce.2
where the time goes:
time: 546 us; the launch traced here: 544 us
  waiting for transfers between devices  228 us (42%)
  matrix products  198 us (36%)
  local copies, waits for them, and re-layouts  95.4 us (17%)
  between operations  14.6 us (3%)
  other arithmetic  7.94 us (1%)
    psum x1, waiting for transfers between devices, on_device(): grad_first = lax.psum(grad_first, ('row', 'col'))  146 us
    dot_general x5, matrix products, add_block(): jnp.einsum('kc,kuf->cuf', selector, contrib, precision=lax.Precision.HIGH...  130 us
    dot_general x5, matrix products, add_block(): jnp.einsum('ktu,ktf->kuf', tile_part, gathered_rows, preferred_element_ty...  64.1 us
    reduce_scatter x1, waiting for transfers between devices, on_device(): lax.psum_scatter(summed_tiles.reshape(col_count * tile_size, features), '...  50.9 us
    gather x5, local copies, waits for them, and re-layouts, add_block(): gathered_rows = buffer_tiles[row_part]  43.7 us
    unnamed x23, local copies, waits for them, and re-layouts  39.7 us
    all_gather x1, waiting for transfers between devices, on_device(): gathered = lax.all_gather(message, 'col', axis=0, tiled=True)  30.8 us
  transfers between devices with their start and end apart: 3, of which 3 were waited for; matrix products, arithmetic and copies ran while one was open for 6% of the time, Pallas kernels for 0%

commit v1 on v0

--- a/solution.py
+++ b/solution.py
@@ -56,7 +56,9 @@
     message = lax.dot_general(
         dpre_two, weight_two, (((1,), (1,)), ((), ())), preferred_element_type=jnp.float32
     ).astype(jnp.bfloat16)
-    gathered = lax.all_gather(message, "col", axis=0, tiled=True)
+    gathered = jnp.concatenate(
+        lax.all_to_all(jnp.stack([message] * lax.axis_size("col")), "col", 0, 0), axis=0
+    )
     buffer_tiles = gathered.reshape(sources * tiles_dev, tile_size, features)
     need_flat = need_rows[0].reshape(-1)
     slot_ids = jnp.arange(sources * slot_count, dtype=jnp.int32)

time: 546 us -> 559 us (1.024)
  starting transfers between devices: 0.12 us -> 8.52 us
    all_gather x1 -> x0, waiting for transfers between devices: 30.8 us -> none  [on_device(): gathered = lax.all_gather(message, 'col', axis=0, tiled=True)]
    all_to_all x0 -> x1, waiting for transfers between devices: none -> 23.8 us  [on_device(): lax.all_to_all(jnp.stack([message] * lax.axis_size('col')), 'col', 0, 0)]
    reduce_scatter x1, waiting for transfers between devices: 50.9 us -> 60.2 us  [on_device(): lax.psum_scatter(summed_tiles.reshape(col_count * tile_size, features), '...]
    all_to_all x0 -> x1, starting transfers between devices: none -> 8.44 us  [on_device(): lax.all_to_all(jnp.stack([message] * lax.axis_size('col')), 'col', 0, 0)]
    unnamed x23 -> x27, local copies, waits for them, and re-layouts: 39.7 us -> 40.4 us
  transfers between devices with their start and end apart: 3 -> 3, of which waited for: 3 -> 3; matrix products, arithmetic and copies ran while one was open for 6% -> 5% of each run, Pallas kernels for 0% -> 0%
where the time goes in v1:
time: 559 us; the launch traced here: 558 us
  waiting for transfers between devices  231 us (41%)
  matrix products  197 us (35%)
  local copies, waits for them, and re-layouts  98.5 us (18%)
  between operations  14.9 us (3%)
  starting transfers between devices  8.52 us (2%)
  other arithmetic  7.94 us (1%)
    psum x1, waiting for transfers between devices, on_device(): grad_first = lax.psum(grad_first, ('row', 'col'))  146 us
    dot_general x5, matrix products, add_block(): jnp.einsum('kc,kuf->cuf', selector, contrib, precision=lax.Precision.HIGH...  130 us
    dot_general x5, matrix products, add_block(): jnp.einsum('ktu,ktf->kuf', tile_part, gathered_rows, preferred_element_ty...  64.2 us
    reduce_scatter x1, waiting for transfers between devices, on_device(): lax.psum_scatter(summed_tiles.reshape(col_count * tile_size, features), '...  60.2 us
    gather x5, local copies, waits for them, and re-layouts, add_block(): gathered_rows = buffer_tiles[row_part]  43.7 us
    unnamed x27, local copies, waits for them, and re-layouts  40.4 us
    all_to_all x1, waiting for transfers between devices, on_device(): lax.all_to_all(jnp.stack([message] * lax.axis_size('col')), 'col', 0, 0)  23.8 us
  transfers between devices with their start and end apart: 3, of which 3 were waited for; matrix products, arithmetic and copies ran while one was open for 5% of the time, Pallas kernels for 0%

profile of v1, /device:TPU:1, one launch (start us, length us, event | category | flops | bytes accessed | tf_op | source)
XLA Modules:
  0.0 558.0 jit_solution(15808698724482401553)
XLA Ops:
  7.2 0.0 copy-start
  7.2 0.0 copy-start.6
  7.2 1.0 copy-done
  8.2 1.2 fusion.22
  9.5 0.2 copy.43
  9.7 0.7 compare_select_fusion.1
  10.4 1.6 gather_fusion.1
  11.9 0.2 copy.44
  12.1 0.1 copy.42
  12.3 0.0 copy-start.4
  12.3 0.1 fusion.20
  12.5 0.2 broadcast_multiply_fusion
  12.6 0.2 copy.46
  12.8 0.2 copy.47
  13.1 3.5 scatter_fusion
  16.6 0.2 copy.48
  16.8 0.2 multiply_convert_fusion.1
  17.0 0.7 copy-done.1
  17.7 0.3 convolution_convert_fusion
  18.0 2.4 stack.2
  20.4 8.4 %all-to-all-start = ((bf16[16,512,256]{2,1,0:T(8,128)(2,1)}), bf16[16,512,256]{2,1,0:T(8,128)(2,1)}, u32[]{:S(2)}, u32[]{:S(2)}) async-start(bf16[16,512,256]{2,1,0:T(8,128)(2,1)} %stack.2), calls=%async_computation | async-start | bytes 8388608 | tf_op jit(solution)/shard_map/all_to_all | solution.py:60
  28.8 0.0 reduce-scatter.2.cloned.1.call-start
  28.9 0.0 copy-start.5
  28.9 27.9 %copy.40 = bf16[640,128,128]{1,2,0:T(8,128)(2,1)} copy(bf16[640,128,128]{2,1,0:T(8,128)(2,1)} %param.19) | data formatting | bytes 41943040 | tf_op args[6]
  56.8 0.1 copy.41
  56.9 0.1 broadcast_in_dim.48
  57.6 0.1 select_reduce_fusion
  57.7 23.8 %all-to-all-done = bf16[16,512,256]{2,1,0:T(8,128)(2,1)} async-done(((bf16[16,512,256]{2,1,0:T(8,128)(2,1)}), bf16[16,512,256]{2,1,0:T(8,128)(2,1)}, u32[]{:S(2)}, u32[]{:S(2)}) %all-to-all-start) | async-done | bytes 4194336 | tf_op jit(solution)/shard_map/all_to_all | solution.py:60
  81.6 241.1 %while.11 = (s32[]{:T(128)}, f32[32,128,256]{2,0,1:T(8,128)}, s32[5,128]{1,0:T(8,128)}, f32[5,128]{1,0:T(8,128)S(1)}, bf16[5,128,128,128]{2,3,1,0:T(8,128)(2,1)}...) while((s32[]{:T(128)}, f32[32,128,256]{2,0,1:T(8,128)}, ...), condition=%wide.region_5.6_spmd.clone, body=%wide.region_4.5_spmd.clone.sunk | while | flops 2686461440 | bytes 71313008 | solution.py:91
  81.6 8.7 %gather_fusion = bf16[128,128,256]{2,1,0:T(8,128)(2,1)} fusion(bf16[64,128,256]{2,1,0:T(8,128)(2,1)} %get-tuple-element.172, s32[1024]{0:T(1024)S(1)} %pad_clamp_fusion.3), kind=kCustom, calls=%fused_computation.clone.clone.1 | custom fusion | bytes 16777728 | tf_op jit(solution)/shard_map/while/body/eval_jaxpr/gather | solution.py:76
  90.3 12.8 %fusion.55 = f32[128,128,256]{2,1,0:T(8,128)} fusion(bf16[128,128,256]{2,1,0:T(8,128)(2,1)} %gather_fusion, bf16[5,128,128,128]{2,3,1,0:T(8,128)(2,1)} %get-tuple-element.170, s32[]{:T(128)} %get-tuple-element.157), kind=kOutput, calls=%fused_computation.6.clone.1 | convolution fusion | flops 1073741824 | bytes 29360640 | tf_op jit(solution)/shard_map/while/body/eval_jaxpr/ktu,ktf->kuf/dot_general | solution.py:77
  103.1 0.7 fusion.57
  103.8 25.4 %select_add_fusion.2 = f32[32,128,256]{2,0,1:T(8,128)} fusion(f32[32,128,256]{2,0,1:T(8,128)} %get-tuple-element.158, pred[]{:T(512)S(6)} %compare.5, f32[128,128,256]{2,1,0:T(8,128)} %fusion.55, f32[128]{0:T(128)S(1)} %fusion.56, s32[128]{0:T(128)S(1)} %fusion.57), kind=kOutput, calls=%fused_computation.8.clone.1 | convolution fusion | flops 1612718080 | bytes 25166848 | tf_op jit(solution)/shard_map/while/body/eval_jaxpr/kc,kuf->cuf/dot_general | solution.py:81
  129.3 8.7 %gather_fusion = bf16[128,128,256]{2,1,0:T(8,128)(2,1)} fusion(bf16[64,128,256]{2,1,0:T(8,128)(2,1)} %get-tuple-element.172, s32[1024]{0:T(1024)S(1)} %pad_clamp_fusion.3), kind=kCustom, calls=%fused_computation.clone.clone.1 | custom fusion | bytes 16777728 | tf_op jit(solution)/shard_map/while/body/eval_jaxpr/gather | solution.py:76
  138.0 12.8 %fusion.55 = f32[128,128,256]{2,1,0:T(8,128)} fusion(bf16[128,128,256]{2,1,0:T(8,128)(2,1)} %gather_fusion, bf16[5,128,128,128]{2,3,1,0:T(8,128)(2,1)} %get-tuple-element.170, s32[]{:T(128)} %get-tuple-element.157), kind=kOutput, calls=%fused_computation.6.clone.1 | convolution fusion | flops 1073741824 | bytes 29360640 | tf_op jit(solution)/shard_map/while/body/eval_jaxpr/ktu,ktf->kuf/dot_general | solution.py:77
  150.9 0.7 fusion.57
  151.6 26.0 %select_add_fusion.2 = f32[32,128,256]{2,0,1:T(8,128)} fusion(f32[32,128,256]{2,0,1:T(8,128)} %get-tuple-element.158, pred[]{:T(512)S(6)} %compare.5, f32[128,128,256]{2,1,0:T(8,128)} %fusion.55, f32[128]{0:T(128)S(1)} %fusion.56, s32[128]{0:T(128)S(1)} %fusion.57), kind=kOutput, calls=%fused_computation.8.clone.1 | convolution fusion | flops 1612718080 | bytes 25166848 | tf_op jit(solution)/shard_map/while/body/eval_jaxpr/kc,kuf->cuf/dot_general | solution.py:81
  177.6 8.7 %gather_fusion = bf16[128,128,256]{2,1,0:T(8,128)(2,1)} fusion(bf16[64,128,256]{2,1,0:T(8,128)(2,1)} %get-tuple-element.172, s32[1024]{0:T(1024)S(1)} %pad_clamp_fusion.3), kind=kCustom, calls=%fused_computation.clone.clone.1 | custom fusion | bytes 16777728 | tf_op jit(solution)/shard_map/while/body/eval_jaxpr/gather | solution.py:76
  186.4 12.8 %fusion.55 = f32[128,128,256]{2,1,0:T(8,128)} fusion(bf16[128,128,256]{2,1,0:T(8,128)(2,1)} %gather_fusion, bf16[5,128,128,128]{2,3,1,0:T(8,128)(2,1)} %get-tuple-element.170, s32[]{:T(128)} %get-tuple-element.157), kind=kOutput, calls=%fused_computation.6.clone.1 | convolution fusion | flops 1073741824 | bytes 29360640 | tf_op jit(solution)/shard_map/while/body/eval_jaxpr/ktu,ktf->kuf/dot_general | solution.py:77
  199.2 0.7 fusion.57
  199.9 26.0 %select_add_fusion.2 = f32[32,128,256]{2,0,1:T(8,128)} fusion(f32[32,128,256]{2,0,1:T(8,128)} %get-tuple-element.158, pred[]{:T(512)S(6)} %compare.5, f32[128,128,256]{2,1,0:T(8,128)} %fusion.55, f32[128]{0:T(128)S(1)} %fusion.56, s32[128]{0:T(128)S(1)} %fusion.57), kind=kOutput, calls=%fused_computation.8.clone.1 | convolution fusion | flops 1612718080 | bytes 25166848 | tf_op jit(solution)/shard_map/while/body/eval_jaxpr/kc,kuf->cuf/dot_general | solution.py:81
  226.0 8.7 %gather_fusion = bf16[128,128,256]{2,1,0:T(8,128)(2,1)} fusion(bf16[64,128,256]{2,1,0:T(8,128)(2,1)} %get-tuple-element.172, s32[1024]{0:T(1024)S(1)} %pad_clamp_fusion.3), kind=kCustom, calls=%fused_computation.clone.clone.1 | custom fusion | bytes 16777728 | tf_op jit(solution)/shard_map/while/body/eval_jaxpr/gather | solution.py:76
  234.7 12.8 %fusion.55 = f32[128,128,256]{2,1,0:T(8,128)} fusion(bf16[128,128,256]{2,1,0:T(8,128)(2,1)} %gather_fusion, bf16[5,128,128,128]{2,3,1,0:T(8,128)(2,1)} %get-tuple-element.170, s32[]{:T(128)} %get-tuple-element.157), kind=kOutput, calls=%fused_computation.6.clone.1 | convolution fusion | flops 1073741824 | bytes 29360640 | tf_op jit(solution)/shard_map/while/body/eval_jaxpr/ktu,ktf->kuf/dot_general | solution.py:77
  247.6 0.7 fusion.57
  248.3 26.0 %select_add_fusion.2 = f32[32,128,256]{2,0,1:T(8,128)} fusion(f32[32,128,256]{2,0,1:T(8,128)} %get-tuple-element.158, pred[]{:T(512)S(6)} %compare.5, f32[128,128,256]{2,1,0:T(8,128)} %fusion.55, f32[128]{0:T(128)S(1)} %fusion.56, s32[128]{0:T(128)S(1)} %fusion.57), kind=kOutput, calls=%fused_computation.8.clone.1 | convolution fusion | flops 1612718080 | bytes 25166848 | tf_op jit(solution)/shard_map/while/body/eval_jaxpr/kc,kuf->cuf/dot_general | solution.py:81
  274.3 8.7 %gather_fusion = bf16[128,128,256]{2,1,0:T(8,128)(2,1)} fusion(bf16[64,128,256]{2,1,0:T(8,128)(2,1)} %get-tuple-element.172, s32[1024]{0:T(1024)S(1)} %pad_clamp_fusion.3), kind=kCustom, calls=%fused_computation.clone.clone.1 | custom fusion | bytes 16777728 | tf_op jit(solution)/shard_map/while/body/eval_jaxpr/gather | solution.py:76
  283.1 12.8 %fusion.55 = f32[128,128,256]{2,1,0:T(8,128)} fusion(bf16[128,128,256]{2,1,0:T(8,128)(2,1)} %gather_fusion, bf16[5,128,128,128]{2,3,1,0:T(8,128)(2,1)} %get-tuple-element.170, s32[]{:T(128)} %get-tuple-element.157), kind=kOutput, calls=%fused_computation.6.clone.1 | convolution fusion | flops 1073741824 | bytes 29360640 | tf_op jit(solution)/shard_map/while/body/eval_jaxpr/ktu,ktf->kuf/dot_general | solution.py:77
  295.9 0.7 fusion.57
  296.6 26.0 %select_add_fusion.2 = f32[32,128,256]{2,0,1:T(8,128)} fusion(f32[32,128,256]{2,0,1:T(8,128)} %get-tuple-element.158, pred[]{:T(512)S(6)} %compare.5, f32[128,128,256]{2,1,0:T(8,128)} %fusion.55, f32[128]{0:T(128)S(1)} %fusion.56, s32[128]{0:T(128)S(1)} %fusion.57), kind=kOutput, calls=%fused_computation.8.clone.1 | convolution fusion | flops 1612718080 | bytes 25166848 | tf_op jit(solution)/shard_map/while/body/eval_jaxpr/kc,kuf->cuf/dot_general | solution.py:81
  322.6 5.9 %copy.49 = f32[32,128,256]{1,0,2:T(8,128)} copy(f32[32,128,256]{2,0,1:T(8,128)} %get-tuple-element.45) | data formatting | bytes 8388608 | tf_op jit(solution)/shard_map/while | solution.py:91
  328.6 8.0 %copy.62 = f32[32,8,32,128]{3,1,2,0:T(8,128)} copy(f32[32,8,32,128]{3,2,1,0:T(8,128)} %bitcast.61) | data formatting | bytes 8388608
  336.6 0.0 reduce-scatter.2.cloned.1.call-update
  336.6 0.0 all-reduce.3.cloned.1.call-start
  336.7 0.9 convolution_bitcast_fusion
  337.6 60.2 %reduce-scatter.2.cloned.1.call-done = f32[512,256]{0,1:T(8,128)} async-done(((f32[4096,256]{0,1:T(8,128)}), f32[512,256]{0,1:T(8,128)}) %reduce-scatter.2.cloned.1.call-update) | async-done | bytes 524304 | tf_op jit(solution)/shard_map/reduce_scatter | solution.py:101
  397.9 1.1 convert_element_type.26
  399.0 1.2 convolution_bitcast_fusion.1
  400.2 0.0 all-reduce.3.cloned.1.call-update
  400.2 0.8 copy.52
  401.0 146.5 %all-reduce.3.cloned.1.call-done = (f32[256,256]{0,1:T(8,128)}, f32[256,256]{0,1:T(8,128)}) async-done(((f32[256,256]{0,1:T(8,128)}, f32[256,256]{0,1:T(8,128)}), (f32[256,256]{0,1:T(8,128)}, f32[256,256]{0,1:T(8,128)})) %all-reduce.3.cloned.1.call-update) | async-done | bytes 524304 | tf_op jit(solution)/shard_map/psum | solution.py:111
  547.5 1.0 broadcast_multiply_fusion.2
  548.5 0.8 copy.53
  549.3 1.0 broadcast_multiply_fusion.1
  550.3 0.8 copy.54
  (34 shorter events, 0.2 us)
Async XLA Ops:
  7.2 1.0 copy-start
  7.2 5.9 %copy-start.6 = (s32[512]{0:T(512)S(1)}, s32[512]{0:T(512)}, u32[]{:S(2)}) copy-start(s32[512]{0:T(512)} %param.16) | copy-start | bytes 6148
  7.2 4.9 copy-start.3
  12.3 5.4 copy-start.4
  17.0 0.7 copy-start.1
  20.4 61.2 %all-to-all-start = ((bf16[16,512,256]{2,1,0:T(8,128)(2,1)}), bf16[16,512,256]{2,1,0:T(8,128)(2,1)}, u32[]{:S(2)}, u32[]{:S(2)}) async-start(bf16[16,512,256]{2,1,0:T(8,128)(2,1)} %stack.2), calls=%async_computation | async-start | bytes 8388608 | tf_op jit(solution)/shard_map/all_to_all | solution.py:60
  28.8 369.0 %reduce-scatter.2.cloned.1.call-start = ((), (), s32[]{:S(2)}) async-start(), calls=%async_computation.2 | async-start | bytes 4718592 | tf_op jit(solution)/shard_map/reduce_scatter | solution.py:101
  28.9 27.9 %copy-start.7 = (s32[1,16,2]{1,2,0:T(2,128)S(1)}, s32[1,16,2]{1,2,0:T(2,128)}, u32[]{:S(2)}) copy-start(s32[1,16,2]{1,2,0:T(2,128)} %param.23) | copy-start | bytes 388
  28.9 28.7 %copy-start.5 = (s32[640]{0:T(1024)S(1)}, s32[640]{0:T(1024)}, u32[]{:S(2)}) copy-start(s32[640]{0:T(1024)} %param.20) | copy-start | bytes 7684
  328.6 8.1 %copy-start.2 = (bf16[512,256]{0,1:T(8,128)(2,1)S(1)}, bf16[512,256]{0,1:T(8,128)(2,1)}, u32[]{:S(2)}) copy-start(bf16[512,256]{0,1:T(8,128)(2,1)} %copy-done.1) | copy-start | bytes 786436
  328.6 70.4 %copy-start.8 = (bf16[512,256]{1,0:T(8,128)(2,1)S(1)}, bf16[512,256]{1,0:T(8,128)(2,1)}, u32[]{:S(2)}) copy-start(bf16[512,256]{1,0:T(8,128)(2,1)} %param.13) | copy-start | bytes 786436
  328.6 70.4 %copy-start.9 = (bf16[256,256]{1,0:T(8,128)(2,1)S(1)}, bf16[256,256]{1,0:T(8,128)(2,1)}, u32[]{:S(2)}) copy-start(bf16[256,256]{1,0:T(8,128)(2,1)} %param.17) | copy-start | bytes 393220
  336.6 210.9 %all-reduce.3.cloned.1.call-start = ((), (), s32[]{:S(2)}) async-start(), calls=%async_computation.3 | async-start | bytes 1048576 | tf_op jit(solution)/shard_map/psum | solution.py:111
Sparse Core Ops, SparseCore 0:
  336.8 61.0 reduce-scatter.1
  403.4 144.0 all-reduce.2
